TPU v7x, 32 devices: a whole 2x2x4 slice. The times are simulated.
32 devices in a mesh: dp: 4 (over z), mp: 8 (over y, x, core).
Axes of the slice: x: 2, y: 2, z: 4, core: 2. Of those that a mesh axis runs over, the one named last changes fastest.
Arguments:
- block_input: bfloat16 [8192, 2048], P(('dp', 'mp')), may hold values from -6 to 6
- out_cotangent: bfloat16 [8192, 2048], P(('dp', 'mp')), may hold values from -6 to 6
- objective: int32 [16], P('dp'), may hold values from 0 to 1, as said below
- prefix_len: int32 [16], P('dp'), may hold values from 64 to 511
- target_mask: int32 [8192], P(('dp', 'mp')), may hold values from 0 to 1, as said below
- qkv_weight: float32 [2048, 3, 2048], P('dp', None, 'mp'), may hold values from -0.125 to 0.125
- out_weight: float32 [2048, 2048], P('mp', 'dp'), may hold values from -3 to 3
- gateup_weight: float32 [2048, 2, 5472], P('dp', None, 'mp'), may hold values from -0.125 to 0.125
- down_weight: float32 [5472, 2048], P('mp', 'dp'), may hold values from -0.625 to 0.625
- norm_params: float32 [4, 2048], replicated, as said below
- qkv_first: float32 [2048, 3, 2048], P('dp', None, 'mp'), may hold values from -0.125 to 0.125
- out_first: float32 [2048, 2048], P('mp', 'dp'), may hold values from -0.005859375 to 0.005859375
- gateup_first: float32 [2048, 2, 5472], P('dp', None, 'mp'), may hold values from -0.09375 to 0.09375
- down_first: float32 [5472, 2048], P('mp', 'dp'), may hold values from -0.013671875 to 0.013671875
- norm_first: float32 [4, 2048], replicated, may hold values from -0.21875 to 0.21875
- qkv_second: float32 [2048, 3, 2048], P('dp', None, 'mp'), may hold values from 3.0517578e-05 to 0.00048828125
- out_second: float32 [2048, 2048], P('mp', 'dp'), may hold values from 7.080078e-08 to 1.1230469e-06
- gateup_second: float32 [2048, 2, 5472], P('dp', None, 'mp'), may hold values from 1.953125e-05 to 0.0003125
- down_second: float32 [5472, 2048], P('mp', 'dp'), may hold values from 4.3945312e-07 to 7.080078e-06
- norm_second: float32 [4, 2048], replicated, may hold values from 0.00012207031 to 0.001953125
Outputs:
- block_output: bfloat16 [8192, 2048], P(('dp', 'mp'))
- input_grad: float32 [8192, 2048], P(('dp', 'mp'))
- qkv_new: float32 [2048, 3, 2048], P('dp', None, 'mp')
- qkv_first_new: float32 [2048, 3, 2048], P('dp', None, 'mp')
- qkv_second_new: float32 [2048, 3, 2048], P('dp', None, 'mp')
- out_new: float32 [2048, 2048], P('mp', 'dp')
- out_first_new: float32 [2048, 2048], P('mp', 'dp')
- out_second_new: float32 [2048, 2048], P('mp', 'dp')
- gateup_new: float32 [2048, 2, 5472], P('dp', None, 'mp')
- gateup_first_new: float32 [2048, 2, 5472], P('dp', None, 'mp')
- gateup_second_new: float32 [2048, 2, 5472], P('dp', None, 'mp')
- down_new: float32 [5472, 2048], P('mp', 'dp')
- down_first_new: float32 [5472, 2048], P('mp', 'dp')
- down_second_new: float32 [5472, 2048], P('mp', 'dp')
- norm_new: float32 [4, 2048], replicated
- norm_first_new: float32 [4, 2048], replicated
- norm_second_new: float32 [4, 2048], replicated
Inputs may be any that keep to these rules, and one draw needn't show every extreme that they name: `objective`: at least one sequence of each kind. `target_mask`: the last residue of every sequence is a target. `norm_params`: rows 0 and 2 are the gains of the first and second norm, rows 1 and 3 their biases.
All inputs are finite; a program needn't handle non-finite values.
Results may differ from a plain program's by a relative error of at most 0.024.
Values may be sent and summed in bfloat16 or wider, within the bound.
No kernel may reach another device: no remote copies, remote signals or barrier semaphores. Data moves between devices by JAX's collectives and lax.ppermute only.
A program may use at most 256 MiB of HBM per device.

v0:
```python
import jax
import jax.numpy as jnp
from jax import lax
from jax.sharding import PartitionSpec as P

D = 2048
HD = 128
FF = 5461
FF_PAD = 5472
STEP = 5
deep_alpha = 48.0**0.5
norm_eps = 1e-05
masked_score = -1e30
rope_base = 10000.0
beta_one = 0.5
beta_two = 0.5
adam_eps = 1e-08
decay_rate = 0.1


def rope_tables(seq_len, head_dim):
    position = jnp.arange(seq_len, dtype=jnp.float32)
    freqs = rope_base ** (-jnp.arange(0, head_dim, 2, dtype=jnp.float32) / head_dim)
    angles = position[:, None] * freqs[None, :]
    return (jnp.cos(angles), jnp.sin(angles))


def rotate(values, cosine, sine_table):
    half_dim = values.shape[-1] // 2
    first_half = values[..., :half_dim]
    second_half = values[..., half_dim:]
    cos_b = cosine[:, None, :]
    sin_b = sine_table[:, None, :]
    return jnp.concatenate(
        [first_half * cos_b - second_half * sin_b, second_half * cos_b + first_half * sin_b], -1
    )


def norm_forward(hidden, norm_gain, norm_bias):
    row_mean = jnp.mean(hidden, -1, keepdims=True)
    centred = hidden - row_mean
    variance = jnp.mean(centred * centred, -1, keepdims=True)
    inv_std = lax.rsqrt(variance + norm_eps)
    normed = centred * inv_std
    return (normed * norm_gain + norm_bias, normed, inv_std)


def norm_backward(grad_rows, normed, inv_std, norm_gain):
    grad_normed = grad_rows * norm_gain
    mean_grad = jnp.mean(grad_normed, -1, keepdims=True)
    mean_proj = jnp.mean(grad_normed * normed, -1, keepdims=True)
    grad_in = inv_std * (grad_normed - mean_grad - normed * mean_proj)
    return (grad_in, jnp.sum(grad_rows * normed, 0), jnp.sum(grad_rows, 0))


def adamw(weight, gradient, first_moment, second, step_rate):
    first_new = beta_one * first_moment + (1.0 - beta_one) * gradient
    second_new = beta_two * second + (1.0 - beta_two) * gradient * gradient
    first_hat = first_new / (1.0 - beta_one**STEP)
    second_hat = second_new / (1.0 - beta_two**STEP)
    weight_new = weight - step_rate * (
        first_hat / (jnp.sqrt(second_hat) + adam_eps) + decay_rate * weight
    )
    return (weight_new, first_new, second_new)


def local(
    block_input,
    out_cotangent,
    objective,
    prefix_len,
    target_mask,
    qkv_weight,
    out_weight,
    gateup_weight,
    down_weight,
    norm_params,
    qkv_first,
    out_first,
    gateup_first,
    down_first,
    norm_first,
    qkv_second,
    out_second,
    gateup_second,
    down_second,
    norm_second,
):
    mp_count = lax.axis_size("mp")
    mp_index = lax.axis_index("mp")
    own_rows = block_input.shape[0]
    seq_count = objective.shape[0]
    group_rows = own_rows * mp_count
    seq_len = group_rows // seq_count
    local_dim = qkv_weight.shape[2]
    local_heads = local_dim // HD
    local_units = gateup_weight.shape[2]
    score_scale = HD ** (-0.5)
    row_start = mp_index * own_rows
    qkv_full, out_full, gateup_full, down_full = (
        lax.all_gather(qkv_weight.astype(jnp.bfloat16), "dp", axis=0, tiled=True),
        lax.all_gather(out_weight.astype(jnp.bfloat16), "dp", axis=1, tiled=True),
        lax.all_gather(gateup_weight.astype(jnp.bfloat16), "dp", axis=0, tiled=True),
        lax.all_gather(down_weight.astype(jnp.bfloat16), "dp", axis=1, tiled=True),
    )
    input_all = lax.all_gather(block_input, "mp", axis=0, tiled=True)
    projected = jnp.einsum("td,dce->tce", input_all, qkv_full, preferred_element_type=jnp.float32)
    shaped = projected.reshape(seq_count, seq_len, 3, local_heads, HD)
    cosine, sine_table = rope_tables(seq_len, HD)
    query_rows = rotate(shaped[:, :, 0], cosine, sine_table).astype(jnp.bfloat16)
    key_rows = rotate(shaped[:, :, 1], cosine, sine_table).astype(jnp.bfloat16)
    value_rows = shaped[:, :, 2].astype(jnp.bfloat16)
    row_index = jnp.arange(seq_len)[:, None]
    col_index = jnp.arange(seq_len)[None, :]
    visible = (
        (objective[:, None, None] > 0)
        | (col_index[None] < prefix_len[:, None, None])
        | (col_index <= row_index)[None]
    )
    scores = (
        jnp.einsum("sihe,sjhe->shij", query_rows, key_rows, preferred_element_type=jnp.float32)
        * score_scale
    )
    scores = jnp.where(visible[:, None], scores, masked_score)
    row_max = jnp.max(scores, -1, keepdims=True)
    exp_scores = jnp.exp(scores - row_max)
    row_total = jnp.sum(exp_scores, -1, keepdims=True)
    soft_weights = exp_scores / row_total
    log_total = row_max + jnp.log(row_total)
    attended = jnp.einsum(
        "shij,sjhe->sihe",
        soft_weights.astype(jnp.bfloat16),
        value_rows,
        preferred_element_type=jnp.float32,
    )
    attended_low = attended.reshape(group_rows, local_dim).astype(jnp.bfloat16)
    attn_part = jnp.dot(attended_low, out_full, preferred_element_type=jnp.float32)
    attn_total = lax.psum(attn_part, "mp")
    hidden_all = deep_alpha * input_all.astype(jnp.float32) + attn_total
    middle_all, _, _ = norm_forward(hidden_all, norm_params[0], norm_params[1])
    middle_low = middle_all.astype(jnp.bfloat16)
    hidden_one = lax.dynamic_slice_in_dim(hidden_all, row_start, own_rows, 0)
    middle = lax.dynamic_slice_in_dim(middle_all, row_start, own_rows, 0)
    live_units = (mp_index * local_units + jnp.arange(local_units) < FF).astype(jnp.float32)
    gate_up = jnp.einsum("td,dcf->tcf", middle_low, gateup_full, preferred_element_type=jnp.float32)
    hidden_low = (jax.nn.gelu(gate_up[:, 0]) * gate_up[:, 1] * live_units).astype(jnp.bfloat16)
    ffn_part = jnp.dot(hidden_low, down_full, preferred_element_type=jnp.float32)
    ffn_total = lax.psum(ffn_part.astype(jnp.bfloat16), "mp").astype(jnp.float32)
    ffn_own = lax.dynamic_slice_in_dim(ffn_total, row_start, own_rows, 0)
    hidden_two = deep_alpha * middle + ffn_own
    output_rows, normed_two, inv_two = norm_forward(hidden_two, norm_params[2], norm_params[3])
    mask_f32 = target_mask.astype(jnp.float32)
    grad_rows = out_cotangent.astype(jnp.float32) * mask_f32[:, None]
    grad_two, gain_two, bias_two = norm_backward(grad_rows, normed_two, inv_two, norm_params[2])
    ffn_back = lax.all_gather(grad_two.astype(jnp.bfloat16), "mp", axis=0, tiled=True)
    gate_again = jnp.einsum(
        "td,dcf->tcf", middle_low, gateup_full, preferred_element_type=jnp.float32
    )
    gate_act, gelu_pull = jax.vjp(jax.nn.gelu, gate_again[:, 0])
    up_part = gate_again[:, 1]
    hidden_again = (gate_act * up_part * live_units).astype(jnp.bfloat16)
    grad_hidden = (
        jnp.einsum("td,fd->tf", ffn_back, down_full, preferred_element_type=jnp.float32)
        * live_units
    )
    down_grad = jnp.einsum("tf,td->fd", hidden_again, ffn_back, preferred_element_type=jnp.float32)
    grad_gate = gelu_pull(grad_hidden * up_part)[0]
    grad_up = grad_hidden * gate_act
    grad_gateup = jnp.stack([grad_gate, grad_up], 1).astype(jnp.bfloat16)
    middle_part = jnp.einsum(
        "tcf,dcf->td", grad_gateup, gateup_full, preferred_element_type=jnp.float32
    )
    gateup_grad = jnp.einsum(
        "td,tcf->dcf", middle_low, grad_gateup, preferred_element_type=jnp.float32
    )
    grad_middle = (
        lax.psum_scatter(
            middle_part.astype(jnp.bfloat16), "mp", scatter_dimension=0, tiled=True
        ).astype(jnp.float32)
        + deep_alpha * grad_two
    )
    _, normed_one, inv_one = norm_forward(hidden_one, norm_params[0], norm_params[1])
    grad_one, gain_one, bias_one = norm_backward(grad_middle, normed_one, inv_one, norm_params[0])
    attn_back = lax.all_gather(grad_one.astype(jnp.bfloat16), "mp", axis=0, tiled=True)
    grad_attended = jnp.einsum(
        "td,ed->te", attn_back, out_full, preferred_element_type=jnp.float32
    ).astype(jnp.bfloat16)
    grad_attended = grad_attended.reshape(seq_count, seq_len, local_heads, HD)
    out_grad = jnp.einsum("te,td->ed", attended_low, attn_back, preferred_element_type=jnp.float32)
    scores_again = (
        jnp.einsum("sihe,sjhe->shij", query_rows, key_rows, preferred_element_type=jnp.float32)
        * score_scale
    )
    scores_again = jnp.where(visible[:, None], scores_again, masked_score)
    soft_again = jnp.exp(scores_again - log_total)
    grad_soft = jnp.einsum(
        "sihe,sjhe->shij", grad_attended, value_rows, preferred_element_type=jnp.float32
    )
    value_grad = jnp.einsum(
        "shij,sihe->sjhe",
        soft_again.astype(jnp.bfloat16),
        grad_attended,
        preferred_element_type=jnp.float32,
    )
    row_dot = jnp.sum(soft_again * grad_soft, -1, keepdims=True)
    grad_scores = (soft_again * (grad_soft - row_dot)).astype(jnp.bfloat16)
    query_grad = (
        jnp.einsum("shij,sjhe->sihe", grad_scores, key_rows, preferred_element_type=jnp.float32)
        * score_scale
    )
    key_grad = (
        jnp.einsum("shij,sihe->sjhe", grad_scores, query_rows, preferred_element_type=jnp.float32)
        * score_scale
    )
    query_lin = rotate(query_grad, cosine, -sine_table)
    key_lin = rotate(key_grad, cosine, -sine_table)
    grad_proj = (
        jnp.stack([query_lin, key_lin, value_grad], 2)
        .astype(jnp.bfloat16)
        .reshape(group_rows, 3, local_dim)
    )
    input_part = jnp.einsum("tce,dce->td", grad_proj, qkv_full, preferred_element_type=jnp.float32)
    qkv_grad = jnp.einsum("td,tce->dce", input_all, grad_proj, preferred_element_type=jnp.float32)
    input_raw = (
        lax.psum_scatter(
            input_part.astype(jnp.bfloat16), "mp", scatter_dimension=0, tiled=True
        ).astype(jnp.float32)
        + deep_alpha * grad_one
    )
    qkv_grad, out_grad, gateup_grad, down_grad = (
        lax.psum_scatter(
            qkv_grad.astype(jnp.bfloat16), "dp", scatter_dimension=0, tiled=True
        ).astype(jnp.float32),
        lax.psum_scatter(
            out_grad.astype(jnp.bfloat16), "dp", scatter_dimension=1, tiled=True
        ).astype(jnp.float32),
        lax.psum_scatter(
            gateup_grad.astype(jnp.bfloat16), "dp", scatter_dimension=0, tiled=True
        ).astype(jnp.float32),
        lax.psum_scatter(
            down_grad.astype(jnp.bfloat16), "dp", scatter_dimension=1, tiled=True
        ).astype(jnp.float32),
    )
    norm_grad = jnp.stack([gain_one, bias_one, gain_two, bias_two], 0)
    norm_grad, target_count = lax.psum((norm_grad, jnp.sum(mask_f32)), ("dp", "mp"))
    rate_list = (D ** (-0.5), 0.5, D ** (-0.5), (FF_PAD // 64) ** (-0.5), 0.4)
    qkv_res = adamw(qkv_weight, qkv_grad / target_count, qkv_first, qkv_second, rate_list[0])
    out_res = adamw(out_weight, out_grad / target_count, out_first, out_second, rate_list[1])
    gateup_res = adamw(
        gateup_weight, gateup_grad / target_count, gateup_first, gateup_second, rate_list[2]
    )
    down_res = adamw(down_weight, down_grad / target_count, down_first, down_second, rate_list[3])
    norm_res = adamw(norm_params, norm_grad / target_count, norm_first, norm_second, rate_list[4])
    return (
        output_rows.astype(jnp.bfloat16),
        input_raw / target_count,
        qkv_res[0],
        qkv_res[1],
        qkv_res[2],
        out_res[0],
        out_res[1],
        out_res[2],
        gateup_res[0],
        gateup_res[1],
        gateup_res[2],
        down_res[0],
        down_res[1],
        down_res[2],
        norm_res[0],
        norm_res[1],
        norm_res[2],
    )


def solution(mesh):
    return jax.shard_map(
        local,
        mesh=mesh,
        in_specs=(
            P(("dp", "mp"), None),
            P(("dp", "mp"), None),
            P("dp"),
            P("dp"),
            P(("dp", "mp")),
            P("dp", None, "mp"),
            P("mp", "dp"),
            P("dp", None, "mp"),
            P("mp", "dp"),
            P(),
            P("dp", None, "mp"),
            P("mp", "dp"),
            P("dp", None, "mp"),
            P("mp", "dp"),
            P(),
            P("dp", None, "mp"),
            P("mp", "dp"),
            P("dp", None, "mp"),
            P("mp", "dp"),
            P(),
        ),
        out_specs=(
            P(("dp", "mp"), None),
            P(("dp", "mp"), None),
            P("dp", None, "mp"),
            P("dp", None, "mp"),
            P("dp", None, "mp"),
            P("mp", "dp"),
            P("mp", "dp"),
            P("mp", "dp"),
            P("dp", None, "mp"),
            P("dp", None, "mp"),
            P("dp", None, "mp"),
            P("mp", "dp"),
            P("mp", "dp"),
            P("mp", "dp"),
            P(),
            P(),
            P(),
        ),
        check_vma=False,
    )
```

profile of v0, /device:TPU:0, one launch (start us, length us, event | category | flops | bytes accessed | tf_op | source)
XLA Modules:
  0.0 1279.1 jit_solution(2433256142239264889)
XLA Ops:
  14.7 61.7 %all-gather.10.cloned.1.call-done = bf16[2048,3,256]{2,0,1:T(8,128)(2,1)} async-done(((bf16[512,3,256]{2,0,1:T(8,128)(2,1)}), bf16[2048,3,256]{2,0,1:T(8,128)(2,1)}) %all-gather.10.cloned.1.call-update) | async-done | bytes 3145744 | tf_op jit(solution)/shard_map/all_gather | solution.py:101
  76.4 54.8 %all-gather.8.cloned.1.call-done = bf16[2048,2048]{1,0:T(8,128)(2,1)} async-done(((bf16[256,2048]{1,0:T(8,128)(2,1)}), bf16[2048,2048]{1,0:T(8,128)(2,1)}) %all-gather.8.cloned.1.call-update) | async-done | bytes 8388624 | tf_op jit(solution)/shard_map/all_gather | solution.py:106
  131.2 11.6 fusion.6
  142.8 8.3 reshape.239
  173.4 11.4 copy.105
  184.8 9.7 fusion.51
  200.8 211.6 %all-reduce.4.cloned.1.call-done = f32[2048,2048]{1,0:T(8,128)} async-done(((f32[2048,2048]{1,0:T(8,128)}), f32[2048,2048]{1,0:T(8,128)}) %all-reduce.4.cloned.1.call-update) | async-done | bytes 16777232 | tf_op jit(solution)/shard_map/psum | solution.py:138
  412.5 16.0 %fusion.81 = (f32[2048]{0:T(1024)S(1)}, f32[2048,2048]{1,0:T(8,128)}) fusion(f32[2048,2048]{1,0:T(8,128)} %all-reduce.4.cloned.1.call-done, bf16[2048,2048]{1,0:T(8,128)(2,1)} %all-gather.8.cloned.1.call-done), kind=kLoop, calls=%fused_computation.166 | loop fusion | flops 16775168 | bytes 41951232 | tf_op jit(solution)/shard_map/reduce_sum | solution.py:40
  428.5 7.7 multiply_reduce_fusion
  436.2 12.2 multiply_add_fusion
  448.5 69.6 %all-gather.14.cloned.1.call-done = bf16[2048,2,684]{0,1,2:T(2,128)(2,1)} async-done(((bf16[512,2,684]{0,1,2:T(2,128)(2,1)}), bf16[2048,2,684]{0,1,2:T(2,128)(2,1)}) %all-gather.14.cloned.1.call-update) | async-done | bytes 5603344 | tf_op jit(solution)/shard_map/all_gather | solution.py:103
  518.1 22.3 %fusion.2 = f32[2048,2,684]{0,2,1:T(8,128)} fusion(bf16[2048,2,684]{0,1,2:T(2,128)(2,1)} %all-gather.14.cloned.1.call-done, f32[2048,2048]{1,0:T(8,128)} %multiply_add_fusion), kind=kOutput, calls=%fused_computation.7 | convolution fusion | flops 11479810048 | bytes 33587200 | tf_op jit(solution)/shard_map/td,dcf->tcf/dot_general | solution.py:145
  545.8 30.5 %all-gather.16.cloned.1.call-done = bf16[684,2048]{1,0:T(8,128)(2,1)} async-done(((bf16[684,512]{1,0:T(8,128)(2,1)}), bf16[684,2048]{1,0:T(8,128)(2,1)}) %all-gather.16.cloned.1.call-update) | async-done | bytes 2801680 | tf_op jit(solution)/shard_map/all_gather | solution.py:104
  576.3 11.2 convolution_convert_fusion
  588.2 124.4 %all-reduce.6.cloned.1.call-done = bf16[2048,2048]{1,0:T(8,128)(2,1)} async-done(((bf16[2048,2048]{1,0:T(8,128)(2,1)}), bf16[2048,2048]{1,0:T(8,128)(2,1)}) %all-reduce.6.cloned.1.call-update) | async-done | bytes 8388624 | tf_op jit(solution)/shard_map/psum | solution.py:148
  719.2 54.5 %all-gather.18.cloned.1.call-done = bf16[2048,2048]{1,0:T(8,128)(2,1)} async-done(((bf16[256,2048]{1,0:T(8,128)(2,1)}), bf16[2048,2048]{1,0:T(8,128)(2,1)}) %all-gather.18.cloned.1.call-update) | async-done | bytes 8388624 | tf_op jit(solution)/shard_map/all_gather | solution.py:155
  773.7 15.4 %fusion.36 = (bf16[2048,1,684]{0,2,1:T(8,128)(2,1)S(1)}, bf16[2048,1,684]{0,2,1:T(8,128)(2,1)S(1)}) fusion(f32[2048,2,684]{0,2,1:T(8,128)} %fusion.2, f32[684]{0:T(1024)S(1)} %fusion.66, bf16[2048,2048]{1,0:T(8,128)(2,1)} %all-gather.18.cloned.1.call-done, bf16[684,2048]{1,0:T(8,128)(2,1)} %all-gather.16.cloned.1.call-done), kind=kOutput, calls=%fused_computation.56 | convolution fusion | flops 5772828672 | bytes 28002992 | tf_op jit(solution)/shard_map/td,fd->tf/dot_general | solution.py:163
  791.6 17.9 %bitcast_convert_fusion.1 = bf16[2048,2048]{1,0:T(8,128)(2,1)} fusion(bf16[2048,2,684]{0,1,2:T(2,128)(2,1)} %all-gather.14.cloned.1.call-done, bf16[2048,1,684]{0,2,1:T(8,128)(2,1)S(1)} %get-tuple-element.102, bf16[2048,1,684]{0,2,1:T(8,128)(2,1)S(1)} %get-tuple-element.101), kind=kOutput, calls=%fused_computation.1 | convolution fusion | flops 11482611712 | bytes 19595264 | tf_op jit(solution)/shard_map/tcf,dcf->td/dot_general | solution.py:170
  813.5 67.7 %reduce-scatter.7.cloned.1.call-done = bf16[256,2048]{1,0:T(8,128)(2,1)} async-done(((bf16[2048,2048]{1,0:T(8,128)(2,1)}), bf16[256,2048]{1,0:T(8,128)(2,1)}) %reduce-scatter.7.cloned.1.call-update) | async-done | bytes 1048592 | tf_op jit(solution)/shard_map/reduce_scatter | solution.py:177
  888.4 18.6 %fusion.19 = bf16[2048,2,684]{0,2,1:T(8,128)(2,1)} fusion(f32[2048,2048]{1,0:T(8,128)} %multiply_add_fusion, bf16[2048,1,684]{0,2,1:T(8,128)(2,1)} %copy-done.49, bf16[2048,1,684]{0,2,1:T(8,128)(2,1)} %copy-done.48), kind=kOutput, calls=%fused_computation.39 | convolution fusion | flops 11493818368 | bytes 27983872 | tf_op jit(solution)/shard_map/td,tcf->dcf/dot_general | solution.py:173
  908.8 10.6 convolution_convert_fusion.1
  920.2 22.6 %all-gather.20.cloned.1.call-done = bf16[2048,2048]{1,0:T(8,128)(2,1)} async-done(((bf16[256,2048]{1,0:T(8,128)(2,1)}), bf16[2048,2048]{1,0:T(8,128)(2,1)}) %all-gather.20.cloned.1.call-update) | async-done | bytes 8388624 | tf_op jit(solution)/shard_map/all_gather | solution.py:184
  942.7 5.8 convolution_convert_fusion.3
  949.6 6.0 fusion.46
  984.3 6.8 convolution_convert_fusion.2
  993.3 12.0 fusion.31
  1007.1 10.8 bitcast_convert_fusion
  1027.8 41.6 %all-reduce = (f32[]{:T(128)}, f32[4,2048]{1,0:T(4,128)S(1)}) all-reduce(f32[]{:T(128)} %convert_reduce_fusion, f32[4,2048]{1,0:T(4,128)S(1)} %pad_maximum_fusion.11), channel_id=1, replica_groups=mesh['dp'=4,'mp'=8] {'dp','mp'}, use_global_device_ids=true, to_apply=%region_18.19 | all-reduce | flops 8193 | bytes 65544 | tf_op jit(solution)/shard_map/psum | solution.py:245
  1087.2 16.2 %reduce-scatter.17.cloned.1.call-done = bf16[684,512]{1,0:T(8,128)(2,1)} async-done(((bf16[684,2048]{1,0:T(8,128)(2,1)}), bf16[684,512]{1,0:T(8,128)(2,1)}) %reduce-scatter.17.cloned.1.call-update) | async-done | bytes 700432 | tf_op jit(solution)/shard_map/reduce_scatter | solution.py:240
  1108.6 24.2 %reduce-scatter.13.cloned.1.call-done = bf16[256,512]{1,0:T(8,128)(2,1)} async-done(((bf16[256,2048]{1,0:T(8,128)(2,1)}), bf16[256,512]{1,0:T(8,128)(2,1)}) %reduce-scatter.13.cloned.1.call-update) | async-done | bytes 262160 | tf_op jit(solution)/shard_map/reduce_scatter | solution.py:234
  1136.4 57.5 %reduce-scatter.11.cloned.1.call-done = bf16[512,3,256]{0,2,1:T(8,128)(2,1)} async-done(((bf16[2048,3,256]{0,2,1:T(8,128)(2,1)}), bf16[512,3,256]{0,2,1:T(8,128)(2,1)}) %reduce-scatter.11.cloned.1.call-update) | async-done | bytes 786448 | tf_op jit(solution)/shard_map/reduce_scatter | solution.py:231
  1208.9 59.7 %reduce-scatter.9.cloned.1.call-done = bf16[256,2048]{1,0:T(8,128)(2,1)} async-done(((bf16[2048,2048]{1,0:T(8,128)(2,1)}), bf16[256,2048]{1,0:T(8,128)(2,1)}) %reduce-scatter.9.cloned.1.call-update) | async-done | bytes 1048592 | tf_op jit(solution)/shard_map/reduce_scatter | solution.py:225
  (208 shorter events, 153.3 us)
Async XLA Ops:
  7.2 6.0 copy-start.47
  7.2 6.0 copy-start.46
  7.2 69.1 %all-gather.10.cloned.1.call-start = ((), (), s32[]{:S(2)}) async-start(), calls=%async_computation.7 | async-start | bytes 3932160 | tf_op jit(solution)/shard_map/all_gather | solution.py:101
  9.7 121.5 %all-gather.8.cloned.1.call-start = ((), (), s32[]{:S(2)}) async-start(), calls=%async_computation.6 | async-start | bytes 9437184 | tf_op jit(solution)/shard_map/all_gather | solution.py:106
  10.5 174.4 %all-gather.12.cloned.1.call-start = ((), (), s32[]{:S(2)}) async-start(), calls=%async_computation.8 | async-start | bytes 1310720 | tf_op jit(solution)/shard_map/all_gather | solution.py:102
  11.3 401.2 %all-reduce.4.cloned.1.call-start = ((), (), s32[]{:S(2)}) async-start(), calls=%async_computation.9 | async-start | bytes 33554432 | tf_op jit(solution)/shard_map/psum | solution.py:138
  13.2 150.0 %copy-start.26 = (f32[512,64]{1,0:T(8,128)}, f32[512,64]{1,0:T(8,128)S(1)}, u32[]{:S(2)}) copy-start(f32[512,64]{1,0:T(8,128)S(1)} %get-tuple-element.124) | copy-start | bytes 393220
  160.7 8.2 copy-start.14
  184.8 9.7 copy-start.1
  194.5 323.5 %all-gather.14.cloned.1.call-start = ((), (), s32[]{:S(2)}) async-start(), calls=%async_computation.10 | async-start | bytes 7004160 | tf_op jit(solution)/shard_map/all_gather | solution.py:103
  198.4 377.9 %all-gather.16.cloned.1.call-start = ((), (), s32[]{:S(2)}) async-start(), calls=%async_computation.11 | async-start | bytes 3522560 | tf_op jit(solution)/shard_map/all_gather | solution.py:104
  200.7 511.8 %all-reduce.6.cloned.1.call-start = ((), (), s32[]{:S(2)}) async-start(), calls=%async_computation.12 | async-start | bytes 16777216 | tf_op jit(solution)/shard_map/psum | solution.py:148
  545.8 41.6 %copy-start.24 = (bf16[2048,684]{0,1:T(8,128)(2,1)}, bf16[2048,684]{0,1:T(8,128)(2,1)S(1)}, u32[]{:S(2)}) copy-start(bf16[2048,684]{0,1:T(8,128)(2,1)S(1)} %multiply_convert_fusion.2) | copy-start | bytes 8404996
  587.5 186.2 %all-gather.18.cloned.1.call-start = ((), (), s32[]{:S(2)}) async-start(), calls=%async_computation.13 | async-start | bytes 9437184 | tf_op jit(solution)/shard_map/all_gather | solution.py:155
  588.2 127.0 %copy-start.20 = (bf16[256,2048]{1,0:T(8,128)(2,1)S(1)}, bf16[256,2048]{1,0:T(8,128)(2,1)}, u32[]{:S(2)}) copy-start(bf16[256,2048]{1,0:T(8,128)(2,1)} %param.21) | copy-start | bytes 3145732
  719.1 162.0 %reduce-scatter.7.cloned.1.call-start = ((), (), s32[]{:S(2)}) async-start(), calls=%async_computation.14 | async-start | bytes 9437184 | tf_op jit(solution)/shard_map/reduce_scatter | solution.py:177
  809.5 133.2 %all-gather.20.cloned.1.call-start = ((), (), s32[]{:S(2)}) async-start(), calls=%async_computation.15 | async-start | bytes 9437184 | tf_op jit(solution)/shard_map/all_gather | solution.py:184
  888.3 181.1 %reduce-scatter.15.cloned.1.call-start = ((), (), s32[]{:S(2)}) async-start(), calls=%async_computation.19 | async-start | bytes 7045120 | tf_op jit(solution)/shard_map/reduce_scatter | solution.py:237
  907.0 196.4 %reduce-scatter.17.cloned.1.call-start = ((), (), s32[]{:S(2)}) async-start(), calls=%async_computation.20 | async-start | bytes 3522560 | tf_op jit(solution)/shard_map/reduce_scatter | solution.py:240
  919.4 23.3 %copy-start.30 = (bf16[256,2048]{1,0:T(8,128)(2,1)S(1)}, bf16[256,2048]{1,0:T(8,128)(2,1)}, u32[]{:S(2)}) copy-start(bf16[256,2048]{1,0:T(8,128)(2,1)} %all-gather.12.cloned.1.call-done) | copy-start | bytes 3145732
  919.5 213.3 %reduce-scatter.13.cloned.1.call-start = ((), (), s32[]{:S(2)}) async-start(), calls=%async_computation.18 | async-start | bytes 1310720 | tf_op jit(solution)/shard_map/reduce_scatter | solution.py:234
  984.3 6.9 copy-start.22
  991.1 202.7 %reduce-scatter.11.cloned.1.call-start = ((), (), s32[]{:S(2)}) async-start(), calls=%async_computation.17 | async-start | bytes 3932160 | tf_op jit(solution)/shard_map/reduce_scatter | solution.py:231
  1005.3 263.3 %reduce-scatter.9.cloned.1.call-start = ((), (), s32[]{:S(2)}) async-start(), calls=%async_computation.16 | async-start | bytes 9437184 | tf_op jit(solution)/shard_map/reduce_scatter | solution.py:225
  1019.4 5.4 copy-start.40
  1019.4 5.4 copy-start.41
  1021.0 48.5 %copy-start.4 = (f32[512,2,684]{0,1,2:T(2,128)S(1)}, f32[512,2,684]{0,1,2:T(2,128)}, u32[]{:S(2)}) copy-start(f32[512,2,684]{0,1,2:T(2,128)} %param.27) | copy-start | bytes 8404996
  1082.1 21.3 %copy-start.19 = (f32[684,512]{1,0:T(8,128)S(1)}, f32[684,512]{1,0:T(8,128)}, u32[]{:S(2)}) copy-start(f32[684,512]{1,0:T(8,128)} %param.28) | copy-start | bytes 4202500
  1082.1 21.3 %copy-start.29 = (f32[684,512]{1,0:T(8,128)S(1)}, f32[684,512]{1,0:T(8,128)}, u32[]{:S(2)}) copy-start(f32[684,512]{1,0:T(8,128)} %param.33) | copy-start | bytes 4202500
  1108.6 85.3 %copy-start.17 = (f32[512,3,256]{0,2,1:T(8,128)S(1)}, f32[512,3,256]{0,2,1:T(8,128)}, u32[]{:S(2)}) copy-start(f32[512,3,256]{0,2,1:T(8,128)} %copy.125) | copy-start | bytes 4718596
  1108.6 85.3 %copy-start.18 = (f32[512,3,256]{0,2,1:T(8,128)S(1)}, f32[512,3,256]{0,2,1:T(8,128)}, u32[]{:S(2)}) copy-start(f32[512,3,256]{0,2,1:T(8,128)} %copy.121) | copy-start | bytes 4718596
  1202.4 66.2 %copy-start.13 = (f32[256,2048]{1,0:T(8,128)S(1)}, f32[256,2048]{1,0:T(8,128)}, u32[]{:S(2)}) copy-start(f32[256,2048]{1,0:T(8,128)} %get-tuple-element.94) | copy-start | bytes 6291460
  (33 other events, 85.8 us)
Sparse Core Ops, SparseCore 0:
  10.2 66.1 all-gather.9
  78.3 52.8 all-gather.7
  133.3 27.9 all-gather.11
  194.6 217.7 all-reduce.3
  414.4 103.5 all-gather.13
  520.0 56.2 all-gather.15
  587.6 124.8 all-reduce.5
  719.3 54.3 all-gather.17
  809.6 71.4 reduce-scatter.6
  888.5 54.2 all-gather.19
  945.1 100.1 reduce-scatter.14
  1047.4 55.9 reduce-scatter.16
  1105.7 26.9 reduce-scatter.12
  1134.9 58.8 reduce-scatter.10
  1197.2 71.3 reduce-scatter.8
where the time goes:
time: 1290 us; the launch traced here: 1280 us
  waiting for transfers between devices  856 us (66%)
  matrix products  171 us (13%)
  other arithmetic  105 us (8%)
  local copies, waits for them, and re-layouts  89.7 us (7%)
  blocking collectives  41.6 us (3%)
  between operations  15 us (1%)
    psum x1, waiting for transfers between devices, local(): attn_total = lax.psum(attn_part, 'mp')  212 us
    psum x1, waiting for transfers between devices, local(): lax.psum(ffn_part.astype(jnp.bfloat16), 'mp').astype(jnp.float32)  124 us
    all_gather x1, waiting for transfers between devices, local(): lax.all_gather(gateup_weight.astype(jnp.bfloat16), 'dp', axis=0, tiled=True)  69.6 us
    reduce_scatter x1, waiting for transfers between devices, local(): lax.psum_scatter(middle_part.astype(jnp.bfloat16), 'mp', scatter_dimensio...  67.7 us
    all_gather x1, waiting for transfers between devices, local(): lax.all_gather(qkv_weight.astype(jnp.bfloat16), 'dp', axis=0, tiled=True)  61.7 us
    reduce_scatter x1, waiting for transfers between devices, local(): lax.psum_scatter(input_part.astype(jnp.bfloat16), 'mp', scatter_dimension...  59.7 us
    reduce_scatter x1, waiting for transfers between devices, local(): lax.psum_scatter(qkv_grad.astype(jnp.bfloat16), 'dp', scatter_dimension=0...  57.5 us
    all_gather x1, waiting for transfers between devices, local(): input_all = lax.all_gather(block_input, 'mp', axis=0, tiled=True)  54.8 us
  transfers between devices with their start and end apart: 15, of which 13 were waited for; matrix products, arithmetic and copies ran while one was open for 22% of the time, Pallas kernels for 0%

commit v1 on v0

--- a/solution.py
+++ b/solution.py
@@ -86,6 +86,18 @@
     down_second,
     norm_second,
 ):
+
+    def view_ports(vals):
+        world = jax.lax.axis_size("mp")
+        reached, n_now = (vals, 0)
+        while 1 << n_now < world:
+            far_arr = jax.lax.ppermute(
+                reached, "mp", [(dd, dd ^ 1 << n_now) for dd in range(world)]
+            )
+            reached = reached + far_arr
+            n_now = n_now + 1
+        return reached
+
     mp_count = lax.axis_size("mp")
     mp_index = lax.axis_index("mp")
     own_rows = block_input.shape[0]
@@ -135,7 +147,7 @@
     )
     attended_low = attended.reshape(group_rows, local_dim).astype(jnp.bfloat16)
     attn_part = jnp.dot(attended_low, out_full, preferred_element_type=jnp.float32)
-    attn_total = lax.psum(attn_part, "mp")
+    attn_total = view_ports(attn_part)
     hidden_all = deep_alpha * input_all.astype(jnp.float32) + attn_total
     middle_all, _, _ = norm_forward(hidden_all, norm_params[0], norm_params[1])
     middle_low = middle_all.astype(jnp.bfloat16)

time: 1290 us -> 1750 us (1.36)
  waiting for transfers between devices: 856 us -> 1280 us
  other arithmetic: 105 us -> 132 us
    ppermute x0 -> x3, waiting for transfers between devices: none -> 738 us  [view_ports(): jax.lax.ppermute(reached, 'mp', [(dd, dd ^ 1 << n_now) for dd in range(wo...]
    psum x1 -> x0, waiting for transfers between devices: 212 us -> none  [local(): attn_total = lax.psum(attn_part, 'mp')]
    all_gather x1, waiting for transfers between devices: 69.6 us -> 0.01 us  [local(): lax.all_gather(gateup_weight.astype(jnp.bfloat16), 'dp', axis=0, tiled=True)]
    all_gather x1, waiting for transfers between devices: 30.5 us -> 0.02 us  [local(): lax.all_gather(down_weight.astype(jnp.bfloat16), 'dp', axis=1, tiled=True)]
    add x0 -> x2, other arithmetic: none -> 23.8 us  [view_ports(): reached = reached + far_arr]
    unnamed x112 -> x116, local copies, waits for them, and re-layouts: 47.2 us -> 50.9 us
  transfers between devices with their start and end apart: 15 -> 17, of which waited for: 13 -> 13; matrix products, arithmetic and copies ran while one was open for 22% -> 16% of each run, Pallas kernels for 0% -> 0%
where the time goes in v1:
time: 1750 us; the launch traced here: 1740 us
  waiting for transfers between devices  1280 us (73%)
  matrix products  166 us (9%)
  other arithmetic  132 us (8%)
  local copies, waits for them, and re-layouts  94.8 us (5%)
  blocking collectives  41.5 us (2%)
    ppermute x3, waiting for transfers between devices, view_ports(): jax.lax.ppermute(reached, 'mp', [(dd, dd ^ 1 << n_now) for dd in range(wo...  738 us
    psum x1, waiting for transfers between devices, local(): lax.psum(ffn_part.astype(jnp.bfloat16), 'mp').astype(jnp.float32)  126 us
    reduce_scatter x1, waiting for transfers between devices, local(): lax.psum_scatter(middle_part.astype(jnp.bfloat16), 'mp', scatter_dimensio...  67.7 us
    all_gather x1, waiting for transfers between devices, local(): lax.all_gather(qkv_weight.astype(jnp.bfloat16), 'dp', axis=0, tiled=True)  61.7 us
    reduce_scatter x1, waiting for transfers between devices, local(): lax.psum_scatter(input_part.astype(jnp.bfloat16), 'mp', scatter_dimension...  59.7 us
    reduce_scatter x1, waiting for transfers between devices, local(): lax.psum_scatter(qkv_grad.astype(jnp.bfloat16), 'dp', scatter_dimension=0...  57.7 us
    all_gather x1, waiting for transfers between devices, local(): input_all = lax.all_gather(block_input, 'mp', axis=0, tiled=True)  54.8 us
    all_gather x1, waiting for transfers between devices, local(): lax.all_gather(grad_two.astype(jnp.bfloat16), 'mp', axis=0, tiled=True)  54.5 us
  transfers between devices with their start and end apart: 17, of which 13 were waited for; matrix products, arithmetic and copies ran while one was open for 16% of the time, Pallas kernels for 0%

profile of v1, /device:TPU:0, one launch (start us, length us, event | category | flops | bytes accessed | tf_op | source)
XLA Modules:
  0.0 1736.5 jit_solution(14238374968244462345)
XLA Ops:
  14.7 61.7 %all-gather.10.cloned.1.call-done = bf16[2048,3,256]{2,0,1:T(8,128)(2,1)} async-done(((bf16[512,3,256]{2,0,1:T(8,128)(2,1)}), bf16[2048,3,256]{2,0,1:T(8,128)(2,1)}) %all-gather.10.cloned.1.call-update) | async-done | bytes 3145744 | tf_op jit(solution)/shard_map/all_gather | solution.py:113
  76.4 54.8 %all-gather.8.cloned.1.call-done = bf16[2048,2048]{1,0:T(8,128)(2,1)} async-done(((bf16[256,2048]{1,0:T(8,128)(2,1)}), bf16[2048,2048]{1,0:T(8,128)(2,1)}) %all-gather.8.cloned.1.call-update) | async-done | bytes 8388624 | tf_op jit(solution)/shard_map/all_gather | solution.py:118
  131.2 11.6 fusion.6
  142.8 8.3 reshape.239
  173.4 12.8 copy.109
  195.9 19.6 %collective-permute-done = f32[2048,2048]{1,0:T(8,128)} collective-permute-done((f32[2048,2048]{1,0:T(8,128)S(1)}, f32[2048,2048]{1,0:T(8,128)}, u32[]{:S(2)}, u32[]{:S(2)}) %collective-permute-start) | collective-permute-done | bytes 16777248 | tf_op jit(solution)/shard_map/ppermute | solution.py:94
  215.5 11.6 add.207
  228.7 361.0 %collective-permute-done.1 = f32[2048,2048]{1,0:T(8,128)} collective-permute-done((f32[2048,2048]{1,0:T(8,128)S(1)}, f32[2048,2048]{1,0:T(8,128)}, u32[]{:S(2)}, u32[]{:S(2)}) %collective-permute-start.1) | collective-permute-done | bytes 16777248 | tf_op jit(solution)/shard_map/ppermute | solution.py:94
  589.8 12.1 add.208
  606.2 357.5 %collective-permute-done.2 = f32[2048,2048]{1,0:T(8,128)} collective-permute-done((f32[2048,2048]{1,0:T(8,128)}, f32[2048,2048]{1,0:T(8,128)}, u32[]{:S(2)}, u32[]{:S(2)}) %collective-permute-start.2) | collective-permute-done | bytes 16777248 | tf_op jit(solution)/shard_map/ppermute | solution.py:94
  963.7 20.6 %fusion.81 = (f32[2048]{0:T(1024)S(1)}, f32[2048,2048]{1,0:T(8,128)}) fusion(f32[2048,2048]{1,0:T(8,128)} %add.208, f32[2048,2048]{1,0:T(8,128)} %collective-permute-done.2, bf16[2048,2048]{1,0:T(8,128)(2,1)} %all-gather.8.cloned.1.call-done), kind=kLoop, calls=%fused_computation.166 | loop fusion | flops 20969472 | bytes 58728448 | tf_op jit(solution)/shard_map/reduce_sum | solution.py:40
  984.4 7.6 multiply_reduce_fusion
  992.0 12.2 multiply_add_fusion
  1004.2 22.3 %fusion.2 = f32[2048,2,684]{0,2,1:T(8,128)} fusion(bf16[2048,2,684]{0,1,2:T(2,128)(2,1)} %all-gather.14.cloned.1.call-done, f32[2048,2048]{1,0:T(8,128)} %multiply_add_fusion), kind=kOutput, calls=%fused_computation.7 | convolution fusion | flops 11479810048 | bytes 33587200 | tf_op jit(solution)/shard_map/td,dcf->tcf/dot_general | solution.py:157
  1032.0 11.7 convolution_convert_fusion
  1044.4 125.7 %all-reduce.3.cloned.1.call-done = bf16[2048,2048]{1,0:T(8,128)(2,1)} async-done(((bf16[2048,2048]{1,0:T(8,128)(2,1)}), bf16[2048,2048]{1,0:T(8,128)(2,1)}) %all-reduce.3.cloned.1.call-update) | async-done | bytes 8388624 | tf_op jit(solution)/shard_map/psum | solution.py:160
  1176.7 54.5 %all-gather.18.cloned.1.call-done = bf16[2048,2048]{1,0:T(8,128)(2,1)} async-done(((bf16[256,2048]{1,0:T(8,128)(2,1)}), bf16[2048,2048]{1,0:T(8,128)(2,1)}) %all-gather.18.cloned.1.call-update) | async-done | bytes 8388624 | tf_op jit(solution)/shard_map/all_gather | solution.py:167
  1231.2 15.4 fusion.36
  1249.1 17.9 %bitcast_convert_fusion.1 = bf16[2048,2048]{1,0:T(8,128)(2,1)} fusion(bf16[2048,2,684]{0,1,2:T(2,128)(2,1)} %all-gather.14.cloned.1.call-done, bf16[2048,1,684]{0,2,1:T(8,128)(2,1)S(1)} %get-tuple-element.102, bf16[2048,1,684]{0,2,1:T(8,128)(2,1)S(1)} %get-tuple-element.101), kind=kOutput, calls=%fused_computation.1 | convolution fusion | flops 11482611712 | bytes 19595264 | tf_op jit(solution)/shard_map/tcf,dcf->td/dot_general | solution.py:182
  1271.0 67.7 %reduce-scatter.7.cloned.1.call-done = bf16[256,2048]{1,0:T(8,128)(2,1)} async-done(((bf16[2048,2048]{1,0:T(8,128)(2,1)}), bf16[256,2048]{1,0:T(8,128)(2,1)}) %reduce-scatter.7.cloned.1.call-update) | async-done | bytes 1048592 | tf_op jit(solution)/shard_map/reduce_scatter | solution.py:189
  1345.9 18.7 %fusion.19 = bf16[2048,2,684]{0,2,1:T(8,128)(2,1)} fusion(f32[2048,2048]{1,0:T(8,128)} %multiply_add_fusion, bf16[2048,1,684]{0,2,1:T(8,128)(2,1)} %copy-done.51, bf16[2048,1,684]{0,2,1:T(8,128)(2,1)} %copy-done.50), kind=kOutput, calls=%fused_computation.39 | convolution fusion | flops 11493818368 | bytes 27983872 | tf_op jit(solution)/shard_map/td,tcf->dcf/dot_general | solution.py:185
  1366.4 10.6 convolution_convert_fusion.1
  1377.8 22.5 %all-gather.20.cloned.1.call-done = bf16[2048,2048]{1,0:T(8,128)(2,1)} async-done(((bf16[256,2048]{1,0:T(8,128)(2,1)}), bf16[2048,2048]{1,0:T(8,128)(2,1)}) %all-gather.20.cloned.1.call-update) | async-done | bytes 8388624 | tf_op jit(solution)/shard_map/all_gather | solution.py:196
  1407.2 6.0 fusion.46
  1441.9 6.8 convolution_convert_fusion.2
  1450.9 12.0 fusion.31
  1464.8 10.8 bitcast_convert_fusion
  1485.5 41.5 %all-reduce = (f32[]{:T(128)}, f32[4,2048]{1,0:T(4,128)S(1)}) all-reduce(f32[]{:T(128)} %convert_reduce_fusion, f32[4,2048]{1,0:T(4,128)S(1)} %pad_maximum_fusion.11), channel_id=1, replica_groups=mesh['dp'=4,'mp'=8] {'dp','mp'}, use_global_device_ids=true, to_apply=%region_17.18 | all-reduce | flops 8193 | bytes 65544 | tf_op jit(solution)/shard_map/psum | solution.py:257
  1544.7 16.2 reduce-scatter.17.cloned.1.call-done
  1566.1 24.0 %reduce-scatter.13.cloned.1.call-done = bf16[256,512]{1,0:T(8,128)(2,1)} async-done(((bf16[256,2048]{1,0:T(8,128)(2,1)}), bf16[256,512]{1,0:T(8,128)(2,1)}) %reduce-scatter.13.cloned.1.call-update) | async-done | bytes 262160 | tf_op jit(solution)/shard_map/reduce_scatter | solution.py:246
  1593.6 57.7 %reduce-scatter.11.cloned.1.call-done = bf16[512,3,256]{0,2,1:T(8,128)(2,1)} async-done(((bf16[2048,3,256]{0,2,1:T(8,128)(2,1)}), bf16[512,3,256]{0,2,1:T(8,128)(2,1)}) %reduce-scatter.11.cloned.1.call-update) | async-done | bytes 786448 | tf_op jit(solution)/shard_map/reduce_scatter | solution.py:243
  1666.4 59.7 %reduce-scatter.9.cloned.1.call-done = bf16[256,2048]{1,0:T(8,128)(2,1)} async-done(((bf16[2048,2048]{1,0:T(8,128)(2,1)}), bf16[256,2048]{1,0:T(8,128)(2,1)}) %reduce-scatter.9.cloned.1.call-update) | async-done | bytes 1048592 | tf_op jit(solution)/shard_map/reduce_scatter | solution.py:237
  (217 shorter events, 168.3 us)
Async XLA Ops:
  7.2 6.0 copy-start.49
  7.2 6.0 copy-start.48
  7.2 69.1 %all-gather.10.cloned.1.call-start = ((), (), s32[]{:S(2)}) async-start(), calls=%async_computation.7 | async-start | bytes 3932160 | tf_op jit(solution)/shard_map/all_gather | solution.py:113
  9.7 121.5 %all-gather.8.cloned.1.call-start = ((), (), s32[]{:S(2)}) async-start(), calls=%async_computation.6 | async-start | bytes 9437184 | tf_op jit(solution)/shard_map/all_gather | solution.py:118
  10.5 175.8 %all-gather.12.cloned.1.call-start = ((), (), s32[]{:S(2)}) async-start(), calls=%async_computation.8 | async-start | bytes 1310720 | tf_op jit(solution)/shard_map/all_gather | solution.py:114
  11.3 992.9 %all-gather.14.cloned.1.call-start = ((), (), s32[]{:S(2)}) async-start(), calls=%async_computation.9 | async-start | bytes 7004160 | tf_op jit(solution)/shard_map/all_gather | solution.py:115
  13.2 150.0 %copy-start.28 = (f32[512,64]{1,0:T(8,128)}, f32[512,64]{1,0:T(8,128)S(1)}, u32[]{:S(2)}) copy-start(f32[512,64]{1,0:T(8,128)S(1)} %get-tuple-element.124) | copy-start | bytes 393220
  160.7 8.2 copy-start.15
  190.2 25.4 %collective-permute-start = (f32[2048,2048]{1,0:T(8,128)S(1)}, f32[2048,2048]{1,0:T(8,128)}, u32[]{:S(2)}, u32[]{:S(2)}) collective-permute-start(f32[2048,2048]{1,0:T(8,128)S(1)} %fusion.51), channel_id=1, source_target_pairs={{0,1},{1,0},{2,3},{3,2},{4,5},{5,4},{6,7},{7,6},{8,9},{9,8},{10,11... | collective-permute-start | bytes 50331656 | tf_op jit(solution)/shard_map/ppermute | solution.py:94
  227.2 375.8 %copy-start.4 = (f32[512,2,684]{0,1,2:T(2,128)S(1)}, f32[512,2,684]{0,1,2:T(2,128)}, u32[]{:S(2)}) copy-start(f32[512,2,684]{0,1,2:T(2,128)} %param.27) | copy-start | bytes 8404996
  227.2 362.6 %collective-permute-start.1 = (f32[2048,2048]{1,0:T(8,128)S(1)}, f32[2048,2048]{1,0:T(8,128)}, u32[]{:S(2)}, u32[]{:S(2)}) collective-permute-start(f32[2048,2048]{1,0:T(8,128)S(1)} %add.207), channel_id=1, source_target_pairs={{0,2},{1,3},{2,0},{3,1},{4,6},{5,7},{6,4},{7,5},{8,10},{9,11},{10,... | collective-permute-start | bytes 50331656 | tf_op jit(solution)/shard_map/ppermute | solution.py:94
  601.9 361.8 %collective-permute-start.2 = (f32[2048,2048]{1,0:T(8,128)}, f32[2048,2048]{1,0:T(8,128)}, u32[]{:S(2)}, u32[]{:S(2)}) collective-permute-start(f32[2048,2048]{1,0:T(8,128)} %add.208), channel_id=1, source_target_pairs={{0,4},{1,5},{2,6},{3,7},{4,0},{5,1},{6,2},{7,3},{8,12},{9,13},{10,... | collective-permute-start | bytes 50331656 | tf_op jit(solution)/shard_map/ppermute | solution.py:94
  605.1 426.9 %all-gather.16.cloned.1.call-start = ((), (), s32[]{:S(2)}) async-start(), calls=%async_computation.10 | async-start | bytes 3522560 | tf_op jit(solution)/shard_map/all_gather | solution.py:116
  606.1 564.0 %all-reduce.3.cloned.1.call-start = ((), (), s32[]{:S(2)}) async-start(), calls=%async_computation.11 | async-start | bytes 16777216 | tf_op jit(solution)/shard_map/psum | solution.py:160
  1031.9 11.8 copy-start.26
  1043.7 187.5 %all-gather.18.cloned.1.call-start = ((), (), s32[]{:S(2)}) async-start(), calls=%async_computation.12 | async-start | bytes 9437184 | tf_op jit(solution)/shard_map/all_gather | solution.py:167
  1044.4 128.3 %copy-start.22 = (bf16[256,2048]{1,0:T(8,128)(2,1)S(1)}, bf16[256,2048]{1,0:T(8,128)(2,1)}, u32[]{:S(2)}) copy-start(bf16[256,2048]{1,0:T(8,128)(2,1)} %param.21) | copy-start | bytes 3145732
  1176.7 162.1 %reduce-scatter.7.cloned.1.call-start = ((), (), s32[]{:S(2)}) async-start(), calls=%async_computation.13 | async-start | bytes 9437184 | tf_op jit(solution)/shard_map/reduce_scatter | solution.py:189
  1267.1 133.3 %all-gather.20.cloned.1.call-start = ((), (), s32[]{:S(2)}) async-start(), calls=%async_computation.14 | async-start | bytes 9437184 | tf_op jit(solution)/shard_map/all_gather | solution.py:196
  1345.9 181.0 %reduce-scatter.15.cloned.1.call-start = ((), (), s32[]{:S(2)}) async-start(), calls=%async_computation.18 | async-start | bytes 7045120 | tf_op jit(solution)/shard_map/reduce_scatter | solution.py:249
  1364.6 196.3 %reduce-scatter.17.cloned.1.call-start = ((), (), s32[]{:S(2)}) async-start(), calls=%async_computation.19 | async-start | bytes 3522560 | tf_op jit(solution)/shard_map/reduce_scatter | solution.py:252
  1377.1 23.3 %copy-start.32 = (bf16[256,2048]{1,0:T(8,128)(2,1)S(1)}, bf16[256,2048]{1,0:T(8,128)(2,1)}, u32[]{:S(2)}) copy-start(bf16[256,2048]{1,0:T(8,128)(2,1)} %all-gather.12.cloned.1.call-done) | copy-start | bytes 3145732
  1377.1 213.0 %reduce-scatter.13.cloned.1.call-start = ((), (), s32[]{:S(2)}) async-start(), calls=%async_computation.17 | async-start | bytes 1310720 | tf_op jit(solution)/shard_map/reduce_scatter | solution.py:246
  1441.9 6.9 copy-start.24
  1448.7 202.6 %reduce-scatter.11.cloned.1.call-start = ((), (), s32[]{:S(2)}) async-start(), calls=%async_computation.16 | async-start | bytes 3932160 | tf_op jit(solution)/shard_map/reduce_scatter | solution.py:243
  1462.9 263.2 %reduce-scatter.9.cloned.1.call-start = ((), (), s32[]{:S(2)}) async-start(), calls=%async_computation.15 | async-start | bytes 9437184 | tf_op jit(solution)/shard_map/reduce_scatter | solution.py:237
  1478.6 48.3 %copy-start.5 = (f32[512,2,684]{0,1,2:T(2,128)S(1)}, f32[512,2,684]{0,1,2:T(2,128)}, u32[]{:S(2)}) copy-start(f32[512,2,684]{0,1,2:T(2,128)} %param.27) | copy-start | bytes 8404996
  1539.6 21.3 %copy-start.21 = (f32[684,512]{1,0:T(8,128)S(1)}, f32[684,512]{1,0:T(8,128)}, u32[]{:S(2)}) copy-start(f32[684,512]{1,0:T(8,128)} %param.28) | copy-start | bytes 4202500
  1539.6 21.3 %copy-start.31 = (f32[684,512]{1,0:T(8,128)S(1)}, f32[684,512]{1,0:T(8,128)}, u32[]{:S(2)}) copy-start(f32[684,512]{1,0:T(8,128)} %param.33) | copy-start | bytes 4202500
  1566.1 85.2 %copy-start.18 = (f32[512,3,256]{0,2,1:T(8,128)S(1)}, f32[512,3,256]{0,2,1:T(8,128)}, u32[]{:S(2)}) copy-start(f32[512,3,256]{0,2,1:T(8,128)} %copy.131) | copy-start | bytes 4718596
  1566.1 85.2 %copy-start.19 = (f32[512,3,256]{0,2,1:T(8,128)S(1)}, f32[512,3,256]{0,2,1:T(8,128)}, u32[]{:S(2)}) copy-start(f32[512,3,256]{0,2,1:T(8,128)} %copy.127) | copy-start | bytes 4718596
  1659.8 66.2 %copy-start.14 = (f32[256,2048]{1,0:T(8,128)S(1)}, f32[256,2048]{1,0:T(8,128)}, u32[]{:S(2)}) copy-start(f32[256,2048]{1,0:T(8,128)} %get-tuple-element.94) | copy-start | bytes 6291460
  (37 other events, 106.4 us)
Sparse Core Ops, SparseCore 0:
  10.2 66.1 all-gather.9
  78.3 52.8 all-gather.7
  133.3 27.9 all-gather.11
  605.2 103.9 all-gather.13
  711.1 56.2 all-gather.15
  1043.8 126.1 all-reduce.2
  1176.8 54.3 all-gather.17
  1267.2 71.4 reduce-scatter.6
  1346.0 54.2 all-gather.19
  1402.5 100.1 reduce-scatter.14
  1505.0 55.8 reduce-scatter.16
  1563.1 26.9 reduce-scatter.12
  1592.4 58.9 reduce-scatter.10
  1654.6 71.3 reduce-scatter.8
